TPU v7x, 256 devices: a whole 4x4x8 slice. The times are simulated.
256 devices in a mesh: section: 16 (over x, z_hi), dp: 16 (over z_lo, y, core).
Axes of the slice: x: 4, y: 4, z: 8 (z_hi: 4, z_lo: 2; z = z_hi * 2 + z_lo), core: 2. Of those that a mesh axis runs over, the one named last changes fastest.
Arguments:
- section_inputs: bfloat16 [16, 768, 1152], P('section'), may hold values from -6 to 6
- mirror_held: bfloat16 [16, 768, 1152], P('section'), may hold values from -6 to 6
- section_cotangents: bfloat16 [16, 768, 1152], P('section'), may hold values from -6 to 6
- next_batch: bfloat16 [768, 1152], replicated, may hold values from -6 to 6
- loss_cotangent: bfloat16 [768, 1152], replicated, may hold values from -6 to 6
- join_weights: bfloat16 [16, 1152, 1152], P('section'), may hold values from -0.125 to 0.125
Outputs:
- section_outputs: bfloat16 [256, 2, 768, 1152], P(('dp', 'section')), parts along dimension 0
- section_gradients: bfloat16 [256, 2, 768, 1152], P(('dp', 'section')), parts along dimension 0
- mirror_arrivals: bfloat16 [256, 768, 1152], P(('dp', 'section')), parts along dimension 0
There are 16 independent parts, one for each index of `dp`. A program takes and returns all parts, laid end to end along the dimension named above; an argument that names none is the same for every part. Nothing has to cross between parts.
All inputs are finite; a program needn't handle non-finite values.
Results may differ from a plain program's by a relative error of at most 0.001.
Values may be sent and summed in bfloat16 or wider, within the bound.
No kernel may reach another device: no remote copies, remote signals or barrier semaphores. Data moves between devices by JAX's collectives and lax.ppermute only.
A program may use at most 128 MiB of HBM per device.

v0:
```python
import jax
import jax.numpy as jnp
from jax import lax
from jax.sharding import PartitionSpec as P


def relay_pairs(count):
    order = list(range(0, count, 2)) + list(range(count - 1, 0, -2))
    return list(zip(order[:-1], order[1:]))


def local(
    section_inputs, mirror_held, section_cotangents, next_batch, loss_cotangent, join_weights
):
    count = lax.axis_size("section")
    replicas = lax.axis_size("dp")
    position = lax.axis_index("section")
    is_early = position % 2 == 0
    weights = join_weights[0]
    rows = next_batch.shape[0] // replicas
    start = lax.axis_index("dp") * rows
    ahead = relay_pairs(count)
    back = [(b, a) for a, b in ahead]
    mirror = [(i, i ^ 1) for i in range(count)]

    def times(left):
        return jnp.dot(left, weights, preferred_element_type=jnp.float32)

    def times_t(left):
        return lax.dot_general(
            left, weights, (((1,), (1,)), ((), ())), preferred_element_type=jnp.float32
        )

    def forward(arriving, pending):
        product = times(arriving)
        joined = (product + pending.astype(jnp.float32)).astype(jnp.bfloat16)
        return (jnp.where(is_early, arriving, joined), product.astype(jnp.bfloat16))

    def backward(cotangent, returned):
        product = times_t(jnp.where(is_early, returned, cotangent))
        return jnp.where(is_early, cotangent.astype(jnp.float32) + product, product).astype(
            jnp.bfloat16
        )

    def part(whole):
        return lax.dynamic_slice_in_dim(whole, start, rows, 0)

    a, held, cot = (section_inputs[0], mirror_held[0], section_cotangents[0])
    a_part, held_part, cot_part = (part(a), part(held), part(cot))
    out_part, skip_part = forward(a_part, held_part)
    grad_part = backward(cot_part, held_part)
    came_out = lax.ppermute(out_part, "section", ahead)
    came_grad = lax.ppermute(grad_part, "section", back)
    came_mirror = lax.ppermute(jnp.where(is_early, skip_part, cot_part), "section", mirror)
    second_in = jnp.where(position == 0, part(next_batch), came_out)
    second_cot = jnp.where(position == 1, part(loss_cotangent), came_grad)
    second_out, second_skip = forward(second_in, came_mirror)
    second_grad = backward(second_cot, came_mirror)
    arrived = lax.ppermute(jnp.where(is_early, second_skip, second_cot), "section", mirror)
    parts = jnp.stack([second_out, second_grad, arrived], axis=0)
    whole = lax.all_gather(parts, "dp", axis=1, tiled=True)
    first_out, _ = forward(a, held)
    first_grad = backward(cot, held)
    section_outputs = jnp.stack([first_out, whole[0]], axis=0)[None]
    section_gradients = jnp.stack([first_grad, whole[1]], axis=0)[None]
    return (section_outputs, section_gradients, whole[2][None])


def solution(mesh):
    in_specs = (
        P("section", None, None),
        P("section", None, None),
        P("section", None, None),
        P(),
        P(),
        P("section", None, None),
    )
    out_specs = (
        P(("dp", "section"), None, None, None),
        P(("dp", "section"), None, None, None),
        P(("dp", "section"), None, None),
    )
    return jax.shard_map(local, mesh=mesh, in_specs=in_specs, out_specs=out_specs, check_vma=False)
```

profile of v0, /device:TPU:1, one launch (start us, length us, event | category | flops | bytes accessed | tf_op | source)
XLA Modules:
  0.0 102.0 jit_solution(10804402269663658548)
XLA Ops:
  7.2 0.0 copy-start
  7.2 0.0 all-gather.2.cloned.1.call-start
  7.2 1.7 %copy-done = bf16[1,1152,1152]{2,1,0:T(8,128)(2,1)S(1)} copy-done((bf16[1,1152,1152]{2,1,0:T(8,128)(2,1)S(1)}, bf16[1,1152,1152]{2,1,0:T(8,128)(2,1)}, u32[]{:S(2)}) %copy-start) | copy-done | bytes 2654232
  8.9 1.9 %fusion.34 = bf16[48,1152]{1,0:T(8,128)(2,1)S(1)} fusion(bf16[1,1152,1152]{2,1,0:T(8,128)(2,1)S(1)} %copy-done, pred[]{:T(512)S(6)} %eq.11, bf16[1,768,1152]{2,1,0:T(8,128)(2,1)} %param.8, s32[]{:T(128)S(6)} %select_n.97, bf16[1,768,1152]{2,1,0:T(8,128)(2,1)} %param.7), kind=kOutput, calls=%fused_computation.29 | convolution fusion | flops 127678464 | bytes 3098624 | tf_op jit(solution)/shard_map/dot_general | solution.py:30
  10.8 1.3 %collective-permute-start.2 = (bf16[48,1152]{1,0:T(8,128)(2,1)S(1)}, bf16[48,1152]{1,0:T(8,128)(2,1)S(1)}, u32[]{:S(2)}, u32[]{:S(2)}) collective-permute-start(bf16[48,1152]{1,0:T(8,128)(2,1)S(1)} %fusion.34), channel_id=1, source_target_pairs={{32,0},{64,32},{96,64},{128,96},{160,128},{192,160},{224,192},{240... | collective-permute-start | bytes 331784 | tf_op jit(solution)/shard_map/ppermute | solution.py:53
  12.1 1.6 %bitcast_select_fusion = (bf16[48,1152]{1,0:T(8,128)(2,1)S(1)}, bf16[48,1152]{1,0:T(8,128)(2,1)S(1)}) fusion(pred[]{:T(512)S(6)} %eq.11, bf16[1,768,1152]{2,1,0:T(8,128)(2,1)} %param.8, s32[]{:T(128)S(6)} %select_n.97, bf16[1,768,1152]{2,1,0:T(8,128)(2,1)} %param.7, bf16[1,768,1152]{2,1,0:T(8,128)(2,1)} %param.6, bf16[1,1152,1152]{2,1,0:T(8,128)(2,1)S(1)} %copy-done), kind=kOutput, calls=%fused_computation.37 | convolution fusion | flops 127733760 | bytes 3319296 | tf_op jit(solution)/shard_map/dot_general | solution.py:27
  13.8 9.6 %collective-permute-start.1 = (bf16[48,1152]{1,0:T(8,128)(2,1)S(1)}, bf16[48,1152]{1,0:T(8,128)(2,1)S(1)}, u32[]{:S(2)}, u32[]{:S(2)}) collective-permute-start(bf16[48,1152]{1,0:T(8,128)(2,1)S(1)} %get-tuple-element.8), channel_id=1, source_target_pairs={{0,16},{16,0},{32,48},{48,32},{64,80},{80,64},{96,112},{112,96},{1... | collective-permute-start | bytes 331784 | tf_op jit(solution)/shard_map/ppermute | solution.py:54
  23.4 3.1 %collective-permute-start = (bf16[48,1152]{1,0:T(8,128)(2,1)S(1)}, bf16[48,1152]{1,0:T(8,128)(2,1)S(1)}, u32[]{:S(2)}, u32[]{:S(2)}) collective-permute-start(bf16[48,1152]{1,0:T(8,128)(2,1)S(1)} %get-tuple-element.9), channel_id=1, source_target_pairs={{0,32},{32,64},{64,96},{96,128},{128,160},{160,192},{192,224},{224... | collective-permute-start | bytes 331784 | tf_op jit(solution)/shard_map/ppermute | solution.py:52
  26.5 0.0 collective-permute-done.2
  26.5 5.1 %collective-permute-done.1 = bf16[48,1152]{1,0:T(8,128)(2,1)S(1)} collective-permute-done((bf16[48,1152]{1,0:T(8,128)(2,1)S(1)}, bf16[48,1152]{1,0:T(8,128)(2,1)S(1)}, u32[]{:S(2)}, u32[]{:S(2)}) %collective-permute-start.1) | collective-permute-done | bytes 110624 | tf_op jit(solution)/shard_map/ppermute | solution.py:54
  31.6 0.0 collective-permute-done
  31.6 1.6 %fusion.39 = (bf16[1,48,1152]{2,1,0:T(8,128)(2,1)S(1)}, bf16[48,1152]{1,0:T(8,128)(2,1)S(1)}) fusion(bf16[48,1152]{1,0:T(8,128)(2,1)S(1)} %collective-permute-done.1, pred[]{:T(512)S(6)} %eq.11, bf16[48,1152]{1,0:T(8,128)(2,1)S(1)} %collective-permute-done, bf16[768,1152]{1,0:T(8,128)(2,1)} %param.9, s32[]{:T(128)S(6)} %select_n.97, pred[]{:T(512)S(6)} %eq.12, ...), kind=kOutput, calls=%fused_computation.34 | convolution fusion | flops 127899648 | bytes 3652608 | tf_op jit(solution)/shard_map/dot_general | solution.py:27
  33.2 6.5 %collective-permute-start.3 = (bf16[48,1152]{1,0:T(8,128)(2,1)S(1)}, bf16[48,1152]{1,0:T(8,128)(2,1)S(1)}, u32[]{:S(2)}, u32[]{:S(2)}) collective-permute-start(bf16[48,1152]{1,0:T(8,128)(2,1)S(1)} %get-tuple-element.7), channel_id=1, source_target_pairs={{0,16},{16,0},{32,48},{48,32},{64,80},{80,64},{96,112},{112,96},{1... | collective-permute-start | bytes 331784 | tf_op jit(solution)/shard_map/ppermute | solution.py:59
  39.7 1.9 %fusion.29 = bf16[1,48,1152]{2,1,0:T(8,128)(2,1)S(1)} fusion(bf16[1,1152,1152]{2,1,0:T(8,128)(2,1)S(1)} %copy-done, bf16[48,1152]{1,0:T(8,128)(2,1)S(1)} %collective-permute-done.1, pred[]{:T(512)S(6)} %eq.11, bf16[48,1152]{1,0:T(8,128)(2,1)S(1)} %collective-permute-done.2, bf16[768,1152]{1,0:T(8,128)(2,1)} %param.10, s32[]{:T(128)S(6)} %select_n.97, ...), kind=kOutput, calls=%fused_computation.27 | convolution fusion | flops 127789056 | bytes 3320832 | tf_op jit(solution)/shard_map/dot_general | solution.py:30
  41.6 3.7 %collective-permute-done.3 = bf16[48,1152]{1,0:T(8,128)(2,1)S(1)} collective-permute-done((bf16[48,1152]{1,0:T(8,128)(2,1)S(1)}, bf16[48,1152]{1,0:T(8,128)(2,1)S(1)}, u32[]{:S(2)}, u32[]{:S(2)}) %collective-permute-start.3) | collective-permute-done | bytes 110624 | tf_op jit(solution)/shard_map/ppermute | solution.py:59
  45.2 0.8 pad_maximum_fusion
  46.0 0.0 all-gather.2.cloned.1.call-update
  46.0 0.0 copy-start.3
  46.0 0.0 copy-start.4
  46.0 6.6 %fusion.3 = bf16[1,768,1152]{2,1,0:T(8,128)(2,1)} fusion(bf16[1,1152,1152]{2,1,0:T(8,128)(2,1)S(1)} %copy-done, bf16[1,768,1152]{2,1,0:T(8,128)(2,1)} %param.7, bf16[1,768,1152]{2,1,0:T(8,128)(2,1)} %param.6, pred[]{:T(512)S(6)} %eq.11), kind=kOutput, calls=%fused_computation.7 | convolution fusion | flops 2041970688 | bytes 7962625 | tf_op jit(solution)/shard_map/dot_general | solution.py:27
  52.6 0.0 copy-done.3
  52.6 0.0 copy-done.4
  52.6 4.0 %fusion.17 = bf16[1,768,1152]{2,1,0:T(8,128)(2,1)} fusion(bf16[1,1152,1152]{2,1,0:T(8,128)(2,1)S(1)} %copy-done, bf16[1,768,1152]{2,1,0:T(8,128)(2,1)S(1)} %copy-done.3, bf16[1,768,1152]{2,1,0:T(8,128)(2,1)S(1)} %copy-done.4, pred[]{:T(512)S(6)} %eq.11), kind=kOutput, calls=%fused_computation.19 | convolution fusion | flops 2042855424 | bytes 7962625 | tf_op jit(solution)/shard_map/dot_general | solution.py:30
  56.6 30.9 %all-gather.2.cloned.1.call-done = bf16[3,768,1152]{2,1,0:T(8,128)(2,1)} async-done(((bf16[3,48,1152]{2,1,0:T(8,128)(2,1)}), bf16[3,768,1152]{2,1,0:T(8,128)(2,1)}) %all-gather.2.cloned.1.call-update) | async-done | bytes 5308432 | tf_op jit(solution)/shard_map/all_gather | solution.py:61
  87.5 0.0 copy-start.1
  87.5 0.0 copy-start.2
  87.5 4.3 %fusion.54 = (bf16[1,768,1152]{2,1,0:T(8,128)(2,1)}, bf16[1,768,1152]{2,1,0:T(8,128)(2,1)S(1)}, bf16[1,768,1152]{2,1,0:T(8,128)(2,1)S(1)}) fusion(bf16[3,768,1152]{2,1,0:T(8,128)(2,1)} %all-gather.2.cloned.1.call-done), kind=kLoop, calls=%fused_computation.53 | loop fusion | bytes 10616832 | tf_op jit(solution)/shard_map/slice | solution.py:66
  91.8 0.0 copy-done.1
  91.8 0.0 copy-done.2
  91.8 3.3 %maximum_bitcast_fusion = (bf16[1,2,768,1152]{3,2,1,0:T(8,128)(2,1)}, bf16[1,2,768,1152]{3,2,1,0:T(8,128)(2,1)}) fusion(bf16[1,768,1152]{2,1,0:T(8,128)(2,1)S(1)} %get-tuple-element.5, bf16[1,768,1152]{2,1,0:T(8,128)(2,1)S(1)} %copy-done.1, bf16[1,768,1152]{2,1,0:T(8,128)(2,1)S(1)} %get-tuple-element.4, bf16[1,768,1152]{2,1,0:T(8,128)(2,1)S(1)} %copy-done.2), kind=kLoop, calls=%fused_computation.3 | loop fusion | flops 3538944 | bytes 14155776 | tf_op jit(solution)/shard_map/broadcast_in_dim | solution.py:64
Async XLA Ops:
  7.2 1.8 %copy-start = (bf16[1,1152,1152]{2,1,0:T(8,128)(2,1)S(1)}, bf16[1,1152,1152]{2,1,0:T(8,128)(2,1)}, u32[]{:S(2)}) copy-start(bf16[1,1152,1152]{2,1,0:T(8,128)(2,1)} %param.11) | copy-start | bytes 7962628
  7.2 80.3 %all-gather.2.cloned.1.call-start = ((), (), s32[]{:S(2)}) async-start(), calls=%async_computation | async-start | bytes 5640192 | tf_op jit(solution)/shard_map/all_gather | solution.py:61
  10.8 15.7 %collective-permute-start.2 = (bf16[48,1152]{1,0:T(8,128)(2,1)S(1)}, bf16[48,1152]{1,0:T(8,128)(2,1)S(1)}, u32[]{:S(2)}, u32[]{:S(2)}) collective-permute-start(bf16[48,1152]{1,0:T(8,128)(2,1)S(1)} %fusion.34), channel_id=1, source_target_pairs={{32,0},{64,32},{96,64},{128,96},{160,128},{192,160},{224,192},{240... | collective-permute-start | bytes 331784 | tf_op jit(solution)/shard_map/ppermute | solution.py:53
  13.8 17.8 %collective-permute-start.1 = (bf16[48,1152]{1,0:T(8,128)(2,1)S(1)}, bf16[48,1152]{1,0:T(8,128)(2,1)S(1)}, u32[]{:S(2)}, u32[]{:S(2)}) collective-permute-start(bf16[48,1152]{1,0:T(8,128)(2,1)S(1)} %get-tuple-element.8), channel_id=1, source_target_pairs={{0,16},{16,0},{32,48},{48,32},{64,80},{80,64},{96,112},{112,96},{1... | collective-permute-start | bytes 331784 | tf_op jit(solution)/shard_map/ppermute | solution.py:54
  23.4 8.2 %collective-permute-start = (bf16[48,1152]{1,0:T(8,128)(2,1)S(1)}, bf16[48,1152]{1,0:T(8,128)(2,1)S(1)}, u32[]{:S(2)}, u32[]{:S(2)}) collective-permute-start(bf16[48,1152]{1,0:T(8,128)(2,1)S(1)} %get-tuple-element.9), channel_id=1, source_target_pairs={{0,32},{32,64},{64,96},{96,128},{128,160},{160,192},{192,224},{224... | collective-permute-start | bytes 331784 | tf_op jit(solution)/shard_map/ppermute | solution.py:52
  33.2 12.1 %collective-permute-start.3 = (bf16[48,1152]{1,0:T(8,128)(2,1)S(1)}, bf16[48,1152]{1,0:T(8,128)(2,1)S(1)}, u32[]{:S(2)}, u32[]{:S(2)}) collective-permute-start(bf16[48,1152]{1,0:T(8,128)(2,1)S(1)} %get-tuple-element.7), channel_id=1, source_target_pairs={{0,16},{16,0},{32,48},{48,32},{64,80},{80,64},{96,112},{112,96},{1... | collective-permute-start | bytes 331784 | tf_op jit(solution)/shard_map/ppermute | solution.py:59
  46.0 6.6 %copy-start.3 = (bf16[1,768,1152]{2,1,0:T(8,128)(2,1)S(1)}, bf16[1,768,1152]{2,1,0:T(8,128)(2,1)}, u32[]{:S(2)}) copy-start(bf16[1,768,1152]{2,1,0:T(8,128)(2,1)} %param.8) | copy-start | bytes 5308420
  46.0 6.6 %copy-start.4 = (bf16[1,768,1152]{2,1,0:T(8,128)(2,1)S(1)}, bf16[1,768,1152]{2,1,0:T(8,128)(2,1)}, u32[]{:S(2)}) copy-start(bf16[1,768,1152]{2,1,0:T(8,128)(2,1)} %param.7) | copy-start | bytes 5308420
  87.5 4.3 %copy-start.1 = (bf16[1,768,1152]{2,1,0:T(8,128)(2,1)S(1)}, bf16[1,768,1152]{2,1,0:T(8,128)(2,1)}, u32[]{:S(2)}) copy-start(bf16[1,768,1152]{2,1,0:T(8,128)(2,1)} %fusion.3) | copy-start | bytes 5308420
  87.5 4.3 %copy-start.2 = (bf16[1,768,1152]{2,1,0:T(8,128)(2,1)S(1)}, bf16[1,768,1152]{2,1,0:T(8,128)(2,1)}, u32[]{:S(2)}) copy-start(bf16[1,768,1152]{2,1,0:T(8,128)(2,1)} %fusion.17) | copy-start | bytes 5308420
Sparse Core Ops, SparseCore 0:
  46.1 41.3 all-gather.1
where the time goes:
time: 102 us
  waiting for transfers between devices  39.7 us (39%)
  starting transfers between devices  20.6 us (20%)
  matrix products  17.5 us (17%)
  between operations  14.1 us (14%)
  local copies, waits for them, and re-layouts  6.01 us (6%)
  other arithmetic  4.11 us (4%)
    all_gather x1, waiting for transfers between devices, local(): whole = lax.all_gather(parts, 'dp', axis=1, tiled=True)  30.9 us
    dot_general x3, matrix products, times(): return jnp.dot(left, weights, preferred_element_type=jnp.float32)  9.78 us
    ppermute x1, starting transfers between devices, local(): lax.ppermute(jnp.where(is_early, skip_part, cot_part), 'section', mirror)  9.63 us
    dot_general x3, matrix products, times_t(): lax.dot_general(left, weights, (((1,), (1,)), ((), ())), preferred_elemen...  7.76 us
    ppermute x1, starting transfers between devices, local(): lax.ppermute(jnp.where(is_early, second_skip, second_cot), 'section', mir...  6.51 us
    ppermute x1, waiting for transfers between devices, local(): lax.ppermute(jnp.where(is_early, skip_part, cot_part), 'section', mirror)  5.07 us
    slice x1, local copies, waits for them, and re-layouts, local(): return (section_outputs, section_gradients, whole[2][None])  4.3 us
    ppermute x1, waiting for transfers between devices, local(): lax.ppermute(jnp.where(is_early, second_skip, second_cot), 'section', mir...  3.65 us
  transfers between devices with their start and end apart: 5, of which 3 were waited for; matrix products, arithmetic and copies ran while one was open for 14% of the time, Pallas kernels for 0%

commit v1 on v0

--- a/solution.py
+++ b/solution.py
@@ -58,7 +58,8 @@
     second_grad = backward(second_cot, came_mirror)
     arrived = lax.ppermute(jnp.where(is_early, second_skip, second_cot), "section", mirror)
     parts = jnp.stack([second_out, second_grad, arrived], axis=0)
-    whole = lax.all_gather(parts, "dp", axis=1, tiled=True)
+    sent = jnp.stack([parts] * lax.axis_size("dp"))
+    whole = jnp.concatenate(lax.all_to_all(sent, "dp", 0, 0), axis=1)
     first_out, _ = forward(a, held)
     first_grad = backward(cot, held)
     section_outputs = jnp.stack([first_out, whole[0]], axis=0)[None]

time: 102 us -> 135 us (1.32)
  the two profiles are of different devices: /device:TPU:1 before, /device:TPU:61 now
where the time goes in v1:
time: 135 us; the launch traced here: 134 us
  waiting for transfers between devices  83.7 us (62%)
  starting transfers between devices  20 us (15%)
  matrix products  17.6 us (13%)
  local copies, waits for them, and re-layouts  8.82 us (7%)
  other arithmetic  3.39 us (3%)
    all_to_all x1, waiting for transfers between devices, local(): whole = jnp.concatenate(lax.all_to_all(sent, 'dp', 0, 0), axis=1)  69.2 us
    dot_general x3, matrix products, times(): return jnp.dot(left, weights, preferred_element_type=jnp.float32)  9.78 us
    ppermute x1, starting transfers between devices, local(): came_grad = lax.ppermute(grad_part, 'section', back)  7.89 us
    ppermute x1, waiting for transfers between devices, local(): lax.ppermute(jnp.where(is_early, skip_part, cot_part), 'section', mirror)  7.81 us
    dot_general x3, matrix products, times_t(): lax.dot_general(left, weights, (((1,), (1,)), ((), ())), preferred_elemen...  7.77 us
    all_to_all x1, starting transfers between devices, local(): whole = jnp.concatenate(lax.all_to_all(sent, 'dp', 0, 0), axis=1)  7.02 us
    slice x1, local copies, waits for them, and re-layouts, local(): return (section_outputs, section_gradients, whole[2][None])  4.31 us
    ppermute x1, starting transfers between devices, local(): came_out = lax.ppermute(out_part, 'section', ahead)  3.69 us
  transfers between devices with their start and end apart: 5, of which 4 were waited for; matrix products, arithmetic and copies ran while one was open for 10% of the time, Pallas kernels for 0%

profile of v1, /device:TPU:61, one launch (start us, length us, event | category | flops | bytes accessed | tf_op | source)
XLA Modules:
  0.0 134.2 jit_solution(12255954918779760592)
XLA Ops:
  0.6 0.0 copy-start
  0.7 1.7 %copy-done = bf16[1,1152,1152]{2,1,0:T(8,128)(2,1)S(1)} copy-done((bf16[1,1152,1152]{2,1,0:T(8,128)(2,1)S(1)}, bf16[1,1152,1152]{2,1,0:T(8,128)(2,1)}, u32[]{:S(2)}) %copy-start) | copy-done | bytes 2654232
  2.4 1.9 %fusion.34 = bf16[48,1152]{1,0:T(8,128)(2,1)S(1)} fusion(bf16[1,1152,1152]{2,1,0:T(8,128)(2,1)S(1)} %copy-done, pred[]{:T(512)S(6)} %eq.11, bf16[1,768,1152]{2,1,0:T(8,128)(2,1)} %param.8, s32[]{:T(128)S(6)} %select_n.97, bf16[1,768,1152]{2,1,0:T(8,128)(2,1)} %param.7), kind=kOutput, calls=%fused_computation.29 | convolution fusion | flops 127678464 | bytes 3098624 | tf_op jit(solution)/shard_map/dot_general | solution.py:30
  4.3 7.9 %collective-permute-start.2 = (bf16[48,1152]{1,0:T(8,128)(2,1)S(1)}, bf16[48,1152]{1,0:T(8,128)(2,1)S(1)}, u32[]{:S(2)}, u32[]{:S(2)}) collective-permute-start(bf16[48,1152]{1,0:T(8,128)(2,1)S(1)} %fusion.34), channel_id=1, source_target_pairs={{32,0},{64,32},{96,64},{128,96},{160,128},{192,160},{224,192},{240... | collective-permute-start | bytes 331784 | tf_op jit(solution)/shard_map/ppermute | solution.py:53
  12.2 1.6 %bitcast_select_fusion = (bf16[48,1152]{1,0:T(8,128)(2,1)S(1)}, bf16[48,1152]{1,0:T(8,128)(2,1)S(1)}) fusion(pred[]{:T(512)S(6)} %eq.11, bf16[1,768,1152]{2,1,0:T(8,128)(2,1)} %param.8, s32[]{:T(128)S(6)} %select_n.97, bf16[1,768,1152]{2,1,0:T(8,128)(2,1)} %param.7, bf16[1,768,1152]{2,1,0:T(8,128)(2,1)} %param.6, bf16[1,1152,1152]{2,1,0:T(8,128)(2,1)S(1)} %copy-done), kind=kOutput, calls=%fused_computation.37 | convolution fusion | flops 127733760 | bytes 3319296 | tf_op jit(solution)/shard_map/dot_general | solution.py:27
  13.8 1.3 collective-permute-start.1
  15.2 3.7 %collective-permute-start = (bf16[48,1152]{1,0:T(8,128)(2,1)S(1)}, bf16[48,1152]{1,0:T(8,128)(2,1)S(1)}, u32[]{:S(2)}, u32[]{:S(2)}) collective-permute-start(bf16[48,1152]{1,0:T(8,128)(2,1)S(1)} %get-tuple-element.9), channel_id=1, source_target_pairs={{0,32},{32,64},{64,96},{96,128},{128,160},{160,192},{192,224},{224... | collective-permute-start | bytes 331784 | tf_op jit(solution)/shard_map/ppermute | solution.py:52
  18.9 0.0 collective-permute-done.2
  18.9 7.8 %collective-permute-done.1 = bf16[48,1152]{1,0:T(8,128)(2,1)S(1)} collective-permute-done((bf16[48,1152]{1,0:T(8,128)(2,1)S(1)}, bf16[48,1152]{1,0:T(8,128)(2,1)S(1)}, u32[]{:S(2)}, u32[]{:S(2)}) %collective-permute-start.1) | collective-permute-done | bytes 110624 | tf_op jit(solution)/shard_map/ppermute | solution.py:54
  26.7 3.7 %collective-permute-done = bf16[48,1152]{1,0:T(8,128)(2,1)S(1)} collective-permute-done((bf16[48,1152]{1,0:T(8,128)(2,1)S(1)}, bf16[48,1152]{1,0:T(8,128)(2,1)S(1)}, u32[]{:S(2)}, u32[]{:S(2)}) %collective-permute-start) | collective-permute-done | bytes 110624 | tf_op jit(solution)/shard_map/ppermute | solution.py:52
  30.4 1.6 %fusion.39 = (bf16[1,48,1152]{2,1,0:T(8,128)(2,1)S(1)}, bf16[48,1152]{1,0:T(8,128)(2,1)S(1)}) fusion(bf16[48,1152]{1,0:T(8,128)(2,1)S(1)} %collective-permute-done.1, pred[]{:T(512)S(6)} %eq.11, bf16[48,1152]{1,0:T(8,128)(2,1)S(1)} %collective-permute-done, bf16[768,1152]{1,0:T(8,128)(2,1)} %param.9, s32[]{:T(128)S(6)} %select_n.97, pred[]{:T(512)S(6)} %eq.12, ...), kind=kOutput, calls=%fused_computation.34 | convolution fusion | flops 127899648 | bytes 3652608 | tf_op jit(solution)/shard_map/dot_general | solution.py:27
  31.9 0.1 collective-permute-start.3
  32.0 1.9 %fusion.29 = bf16[1,48,1152]{2,1,0:T(8,128)(2,1)S(1)} fusion(bf16[1,1152,1152]{2,1,0:T(8,128)(2,1)S(1)} %copy-done, bf16[48,1152]{1,0:T(8,128)(2,1)S(1)} %collective-permute-done.1, pred[]{:T(512)S(6)} %eq.11, bf16[48,1152]{1,0:T(8,128)(2,1)S(1)} %collective-permute-done.2, bf16[768,1152]{1,0:T(8,128)(2,1)} %param.10, s32[]{:T(128)S(6)} %select_n.97, ...), kind=kOutput, calls=%fused_computation.27 | convolution fusion | flops 127789056 | bytes 3320832 | tf_op jit(solution)/shard_map/dot_general | solution.py:30
  33.9 3.0 %collective-permute-done.3 = bf16[48,1152]{1,0:T(8,128)(2,1)S(1)} collective-permute-done((bf16[48,1152]{1,0:T(8,128)(2,1)S(1)}, bf16[48,1152]{1,0:T(8,128)(2,1)S(1)}, u32[]{:S(2)}, u32[]{:S(2)}) %collective-permute-start.3) | collective-permute-done | bytes 110624 | tf_op jit(solution)/shard_map/ppermute | solution.py:59
  37.0 2.8 %stack.23 = bf16[16,3,48,1152]{3,2,1,0:T(8,128)(2,1)} broadcast(bf16[3,48,1152]{2,1,0:T(8,128)(2,1)S(1)} %pad_maximum_fusion), dimensions={1,2,3} | broadcast | bytes 5640192 | tf_op jit(solution)/shard_map/stack | solution.py:61
  39.8 7.0 %all-to-all-start = ((bf16[16,3,48,1152]{3,2,1,0:T(8,128)(2,1)}), bf16[16,3,48,1152]{3,2,1,0:T(8,128)(2,1)}, u32[]{:S(2)}, u32[]{:S(2)}) async-start(bf16[16,3,48,1152]{3,2,1,0:T(8,128)(2,1)} %stack.23), calls=%async_computation | async-start | bytes 10616832 | tf_op jit(solution)/shard_map/all_to_all | solution.py:62
  46.8 0.0 copy-start.3
  46.8 0.0 copy-start.4
  46.8 6.6 %fusion.3 = bf16[1,768,1152]{2,1,0:T(8,128)(2,1)} fusion(bf16[1,1152,1152]{2,1,0:T(8,128)(2,1)S(1)} %copy-done, bf16[1,768,1152]{2,1,0:T(8,128)(2,1)} %param.7, bf16[1,768,1152]{2,1,0:T(8,128)(2,1)} %param.6, pred[]{:T(512)S(6)} %eq.11), kind=kOutput, calls=%fused_computation.7 | convolution fusion | flops 2041970688 | bytes 7962625 | tf_op jit(solution)/shard_map/dot_general | solution.py:27
  53.4 0.0 copy-done.3
  53.4 0.0 copy-done.4
  53.4 4.0 %fusion.17 = bf16[1,768,1152]{2,1,0:T(8,128)(2,1)} fusion(bf16[1,1152,1152]{2,1,0:T(8,128)(2,1)S(1)} %copy-done, bf16[1,768,1152]{2,1,0:T(8,128)(2,1)S(1)} %copy-done.3, bf16[1,768,1152]{2,1,0:T(8,128)(2,1)S(1)} %copy-done.4, pred[]{:T(512)S(6)} %eq.11), kind=kOutput, calls=%fused_computation.19 | convolution fusion | flops 2042855424 | bytes 7962625 | tf_op jit(solution)/shard_map/dot_general | solution.py:30
  57.4 69.2 %all-to-all-done = bf16[16,3,48,1152]{3,2,1,0:T(8,128)(2,1)} async-done(((bf16[16,3,48,1152]{3,2,1,0:T(8,128)(2,1)}), bf16[16,3,48,1152]{3,2,1,0:T(8,128)(2,1)}, u32[]{:S(2)}, u32[]{:S(2)}) %all-to-all-start) | async-done | bytes 5308448 | tf_op jit(solution)/shard_map/all_to_all | solution.py:62
  126.5 0.0 copy-start.1
  126.5 0.0 copy-start.2
  126.5 4.3 %fusion.54 = (bf16[1,16,48,1152]{3,2,0,1:T(8,128)(2,1)}, bf16[1,16,48,1152]{3,2,0,1:T(8,128)(2,1)S(1)}, bf16[1,16,48,1152]{3,2,0,1:T(8,128)(2,1)S(1)}) fusion(bf16[3,16,48,1152]{3,2,0,1:T(8,128)(2,1)} %bitcast.11), kind=kLoop, calls=%fused_computation.53 | loop fusion | bytes 10616832 | tf_op jit(solution)/shard_map/slice | solution.py:67
  130.8 0.0 copy-done.1
  130.8 0.0 copy-done.2
  130.8 3.3 %maximum_bitcast_fusion = (bf16[1,2,768,1152]{3,2,1,0:T(8,128)(2,1)}, bf16[1,2,768,1152]{3,2,1,0:T(8,128)(2,1)}) fusion(bf16[1,768,1152]{2,1,0:T(8,128)(2,1)S(1)} %bitcast.76, bf16[1,768,1152]{2,1,0:T(8,128)(2,1)S(1)} %copy-done.1, bf16[1,768,1152]{2,1,0:T(8,128)(2,1)S(1)} %bitcast.75, bf16[1,768,1152]{2,1,0:T(8,128)(2,1)S(1)} %copy-done.2), kind=kLoop, calls=%fused_computation.3 | loop fusion | flops 3538944 | bytes 14155776 | tf_op jit(solution)/shard_map/broadcast_in_dim | solution.py:65
  (1 shorter events, 0.0 us)
Async XLA Ops:
  0.6 1.8 %copy-start = (bf16[1,1152,1152]{2,1,0:T(8,128)(2,1)S(1)}, bf16[1,1152,1152]{2,1,0:T(8,128)(2,1)}, u32[]{:S(2)}) copy-start(bf16[1,1152,1152]{2,1,0:T(8,128)(2,1)} %param.11) | copy-start | bytes 7962628
  4.3 14.6 %collective-permute-start.2 = (bf16[48,1152]{1,0:T(8,128)(2,1)S(1)}, bf16[48,1152]{1,0:T(8,128)(2,1)S(1)}, u32[]{:S(2)}, u32[]{:S(2)}) collective-permute-start(bf16[48,1152]{1,0:T(8,128)(2,1)S(1)} %fusion.34), channel_id=1, source_target_pairs={{32,0},{64,32},{96,64},{128,96},{160,128},{192,160},{224,192},{240... | collective-permute-start | bytes 331784 | tf_op jit(solution)/shard_map/ppermute | solution.py:53
  13.8 12.8 %collective-permute-start.1 = (bf16[48,1152]{1,0:T(8,128)(2,1)S(1)}, bf16[48,1152]{1,0:T(8,128)(2,1)S(1)}, u32[]{:S(2)}, u32[]{:S(2)}) collective-permute-start(bf16[48,1152]{1,0:T(8,128)(2,1)S(1)} %get-tuple-element.8), channel_id=1, source_target_pairs={{0,16},{16,0},{32,48},{48,32},{64,80},{80,64},{96,112},{112,96},{1... | collective-permute-start | bytes 331784 | tf_op jit(solution)/shard_map/ppermute | solution.py:54
  15.2 15.2 %collective-permute-start = (bf16[48,1152]{1,0:T(8,128)(2,1)S(1)}, bf16[48,1152]{1,0:T(8,128)(2,1)S(1)}, u32[]{:S(2)}, u32[]{:S(2)}) collective-permute-start(bf16[48,1152]{1,0:T(8,128)(2,1)S(1)} %get-tuple-element.9), channel_id=1, source_target_pairs={{0,32},{32,64},{64,96},{96,128},{128,160},{160,192},{192,224},{224... | collective-permute-start | bytes 331784 | tf_op jit(solution)/shard_map/ppermute | solution.py:52
  31.9 5.0 %collective-permute-start.3 = (bf16[48,1152]{1,0:T(8,128)(2,1)S(1)}, bf16[48,1152]{1,0:T(8,128)(2,1)S(1)}, u32[]{:S(2)}, u32[]{:S(2)}) collective-permute-start(bf16[48,1152]{1,0:T(8,128)(2,1)S(1)} %get-tuple-element.7), channel_id=1, source_target_pairs={{0,16},{16,0},{32,48},{48,32},{64,80},{80,64},{96,112},{112,96},{1... | collective-permute-start | bytes 331784 | tf_op jit(solution)/shard_map/ppermute | solution.py:59
  39.8 86.7 %all-to-all-start = ((bf16[16,3,48,1152]{3,2,1,0:T(8,128)(2,1)}), bf16[16,3,48,1152]{3,2,1,0:T(8,128)(2,1)}, u32[]{:S(2)}, u32[]{:S(2)}) async-start(bf16[16,3,48,1152]{3,2,1,0:T(8,128)(2,1)} %stack.23), calls=%async_computation | async-start | bytes 10616832 | tf_op jit(solution)/shard_map/all_to_all | solution.py:62
  46.8 6.6 %copy-start.3 = (bf16[1,768,1152]{2,1,0:T(8,128)(2,1)S(1)}, bf16[1,768,1152]{2,1,0:T(8,128)(2,1)}, u32[]{:S(2)}) copy-start(bf16[1,768,1152]{2,1,0:T(8,128)(2,1)} %param.8) | copy-start | bytes 5308420
  46.8 6.6 %copy-start.4 = (bf16[1,768,1152]{2,1,0:T(8,128)(2,1)S(1)}, bf16[1,768,1152]{2,1,0:T(8,128)(2,1)}, u32[]{:S(2)}) copy-start(bf16[1,768,1152]{2,1,0:T(8,128)(2,1)} %param.7) | copy-start | bytes 5308420
  126.5 4.3 %copy-start.1 = (bf16[1,768,1152]{2,1,0:T(8,128)(2,1)S(1)}, bf16[1,768,1152]{2,1,0:T(8,128)(2,1)}, u32[]{:S(2)}) copy-start(bf16[1,768,1152]{2,1,0:T(8,128)(2,1)} %fusion.3) | copy-start | bytes 5308420
  126.5 4.3 %copy-start.2 = (bf16[1,768,1152]{2,1,0:T(8,128)(2,1)S(1)}, bf16[1,768,1152]{2,1,0:T(8,128)(2,1)}, u32[]{:S(2)}) copy-start(bf16[1,768,1152]{2,1,0:T(8,128)(2,1)} %fusion.17) | copy-start | bytes 5308420
